TPU v7x, 32 devices: a whole 2x2x4 slice. The times are simulated.
32 devices in a mesh: pages: 8 (over z, core), blocks: 4 (over y, x).
Axes of the slice: x: 2, y: 2, z: 4, core: 2. Of those that a mesh axis runs over, the one named last changes fastest.
Arguments:
- queries: bfloat16 [64, 24, 128], P(('pages', 'blocks')), may hold values from -0.5 to 0.5
- centroids: bfloat16 [256, 128], replicated, may hold values from -6 to 6
- basis: bfloat16 [256, 32, 128], replicated, may hold values from -1 to 1
- patch_ids: int32 [8, 32, 256], P('pages', None, 'blocks'), may hold values from 0 to 255
- coeffs: bfloat16 [8, 32, 8192], P('pages', None, 'blocks'), may hold values from -6 to 6
- page_counts: int32 [8, 32], P('pages'), may hold values from 128 to 256
- cand_ids: int32 [8, 64, 16], P('pages'), may hold values from 0 to 31
- cand_counts: int32 [8, 64], P('pages'), may hold values from 0 to 16, as said below
Outputs:
- scores: float32 [64, 8, 16], P(('pages', 'blocks'))
Inputs may be any that keep to these rules, and one draw needn't show every extreme that they name: `cand_ids`: slots at or past a query's count in a group are padding and name arbitrary pages; ids may repeat. `cand_counts`: each query's counts over the 8 groups add up to 64.
All inputs are finite; a program needn't handle non-finite values.
Results may differ from a plain program's by a relative error of at most 0.00065.
Values may be sent and summed in bfloat16 or wider, within the bound.
A program may use at most 64 MiB of HBM per device.

v0:
```python
import math

import jax
import jax.numpy as jnp
from jax import lax
from jax.sharding import PartitionSpec as P


def decode_block(ids_block, coef_block, centroids, basis):
    page_total, patch_total = ids_block.shape
    cent_total, rank_width, width = basis.shape
    flat_ids = ids_block.reshape(-1)
    onehot = (flat_ids[:, None] == jnp.arange(cent_total, dtype=jnp.int32)[None, :]).astype(
        jnp.bfloat16
    )
    center = jnp.dot(onehot, centroids, preferred_element_type=jnp.float32)
    coeff_rows = coef_block.reshape(page_total * patch_total, rank_width)
    weighted = (onehot[:, :, None] * coeff_rows[:, None, :]).reshape(
        page_total * patch_total, cent_total * rank_width
    )
    residual = jnp.dot(
        weighted, basis.reshape(cent_total * rank_width, width), preferred_element_type=jnp.float32
    )
    return (center + residual).astype(jnp.bfloat16).reshape(page_total, patch_total, width)


def on_device(queries, centroids, basis, patch_ids, coeffs, page_counts, cand_ids, cand_counts):
    page_total = patch_ids.shape[1]
    block_len = patch_ids.shape[2]
    page_step = math.gcd(page_total, 8)
    ids_blocks = patch_ids[0].reshape(page_total // page_step, page_step, block_len)
    coef_blocks = coeffs[0].reshape(page_total // page_step, page_step, -1)
    embedded = lax.map(
        lambda inputs: decode_block(inputs[0], inputs[1], centroids, basis),
        (ids_blocks, coef_blocks),
    )
    embedded = embedded.reshape(page_total, block_len, -1)
    patch_pos = lax.axis_index("blocks") * block_len + jnp.arange(block_len, dtype=jnp.int32)
    live_counts = page_counts[0]
    page_index = jnp.arange(page_total, dtype=jnp.int32)
    cand_rows = cand_ids[0]
    cand_live = cand_counts[0]
    slot_count = cand_rows.shape[1]
    piece = lax.all_gather(queries, ("pages", "blocks"), axis=0, tiled=True)
    piece_rows = piece.shape[0]
    group_size = math.gcd(piece_rows, 16)

    def one_block(inputs):
        query_group, cand_group, count_group = inputs
        chosen = jnp.take(embedded, cand_group, axis=0)
        similar = jnp.einsum(
            "gcpd,gtd->gcpt", chosen, query_group, preferred_element_type=jnp.float32
        )
        match_page = cand_group[:, :, None] == page_index[None, None, :]
        cand_patches = jnp.sum(jnp.where(match_page, live_counts[None, None, :], 0), axis=2)
        valid_patch = patch_pos[None, None, :] < cand_patches[:, :, None]
        similar = jnp.where(valid_patch[..., None], similar, -jnp.inf)
        block_best = jnp.max(similar, axis=2)
        slot_used = jnp.arange(slot_count, dtype=jnp.int32)[None, :] < count_group[:, None]
        return jnp.where(slot_used[..., None], block_best, 0.0).astype(jnp.bfloat16)

    turns = piece_rows // group_size
    results = lax.map(
        one_block,
        (
            piece.reshape(turns, group_size, piece.shape[1], piece.shape[2]),
            cand_rows.reshape(turns, group_size, slot_count),
            cand_live.reshape(turns, group_size),
        ),
    )
    block_best = results.reshape(piece_rows, slot_count, -1)
    n_pages = lax.axis_size("pages")
    n_blocks = lax.axis_size("blocks")
    owned = queries.shape[0]
    shaped = block_best.reshape(n_pages, n_blocks, owned, slot_count, block_best.shape[2])
    arrived = lax.all_to_all(
        lax.all_to_all(shaped, "pages", split_axis=0, concat_axis=0, tiled=True),
        "blocks",
        split_axis=1,
        concat_axis=1,
        tiled=True,
    )
    highest = jnp.max(arrived, axis=1)
    totals = jnp.sum(highest.astype(jnp.float32), axis=3) / highest.shape[3]
    return jnp.transpose(totals, (1, 0, 2))


def solution(mesh):
    placed = (
        P(("pages", "blocks"), None, None),
        P(),
        P(),
        P("pages", None, "blocks"),
        P("pages", None, "blocks"),
        P("pages", None),
        P("pages", None, None),
        P("pages", None),
    )
    return jax.shard_map(
        on_device,
        mesh=mesh,
        in_specs=placed,
        out_specs=P(("pages", "blocks"), None, None),
        check_vma=False,
    )
```

profile of v0, /device:TPU:0, one launch (start us, length us, event | category | flops | bytes accessed | tf_op | source)
XLA Modules:
  0.0 150.6 jit_solution(1330549599496086359)
XLA Ops:
  0.0 2.4 %copy.23 = bf16[256,32,128]{2,0,1:T(8,128)(2,1)S(1)} copy(bf16[256,32,128]{2,1,0:T(8,128)(2,1)} %param.14) | data formatting | bytes 4194304 | tf_op jit(solution)/shard_map/while | solution.py:33
  2.5 18.6 %while.21 = (s32[]{:T(128)}, bf16[4,8,64,128]{3,2,1,0:T(8,128)(2,1)S(1)}, s32[4,8,64]{2,1,0:T(8,128)}, bf16[256,128]{1,0:T(8,128)(2,1)S(1)}, bf16[4,8,2048]{2,1,...) while((s32[]{:T(128)}, bf16[4,8,64,128]{3,2,1,0:T(8,128)(2,1)S(1)}, s32[4,8,64]{2,1,0:T(8,128)}, ...), condition=%wide.region_1.2_spmd, body=%wide.region_0.1_spmd.sunk | while | flops 1112014848 | bytes 3846233 | solution.py:33
  2.5 0.7 constant_dynamic-slice_fusion.6
  3.3 0.1 fusion.42
  3.4 0.8 constant_dynamic-slice_fusion.5
  4.2 0.1 mul.42
  4.4 2.4 %fusion.43 = f32[512,128]{1,0:T(8,128)S(1)} fusion(bf16[256,32,128]{2,0,1:T(8,128)(2,1)S(1)} %get-tuple-element.275, bf16[512,32]{0,1:T(8,128)(2,1)S(1)} %copy.30, bf16[512,256]{1,0:T(8,128)(2,1)S(1)} %fusion.42), kind=kOutput, calls=%fused_computation.8.clone.1 | convolution fusion | flops 1077936128 | bytes 2654208 | tf_op jit(solution)/shard_map/while/body/eval_jaxpr/dot_general | solution.py:21
  6.8 0.3 fusion.44
  7.2 0.7 constant_dynamic-slice_fusion.6
  7.9 0.1 fusion.42
  8.1 0.8 constant_dynamic-slice_fusion.5
  8.8 0.1 mul.42
  9.1 2.4 %fusion.43 = f32[512,128]{1,0:T(8,128)S(1)} fusion(bf16[256,32,128]{2,0,1:T(8,128)(2,1)S(1)} %get-tuple-element.275, bf16[512,32]{0,1:T(8,128)(2,1)S(1)} %copy.30, bf16[512,256]{1,0:T(8,128)(2,1)S(1)} %fusion.42), kind=kOutput, calls=%fused_computation.8.clone.1 | convolution fusion | flops 1077936128 | bytes 2654208 | tf_op jit(solution)/shard_map/while/body/eval_jaxpr/dot_general | solution.py:21
  11.5 0.3 fusion.44
  11.8 0.7 constant_dynamic-slice_fusion.6
  12.7 0.8 constant_dynamic-slice_fusion.5
  13.5 0.1 mul.42
  13.7 2.4 %fusion.43 = f32[512,128]{1,0:T(8,128)S(1)} fusion(bf16[256,32,128]{2,0,1:T(8,128)(2,1)S(1)} %get-tuple-element.275, bf16[512,32]{0,1:T(8,128)(2,1)S(1)} %copy.30, bf16[512,256]{1,0:T(8,128)(2,1)S(1)} %fusion.42), kind=kOutput, calls=%fused_computation.8.clone.1 | convolution fusion | flops 1077936128 | bytes 2654208 | tf_op jit(solution)/shard_map/while/body/eval_jaxpr/dot_general | solution.py:21
  16.1 0.3 fusion.44
  16.4 0.7 constant_dynamic-slice_fusion.6
  17.2 0.1 fusion.42
  17.3 0.8 constant_dynamic-slice_fusion.5
  18.1 0.1 mul.42
  18.4 2.4 %fusion.43 = f32[512,128]{1,0:T(8,128)S(1)} fusion(bf16[256,32,128]{2,0,1:T(8,128)(2,1)S(1)} %get-tuple-element.275, bf16[512,32]{0,1:T(8,128)(2,1)S(1)} %copy.30, bf16[512,256]{1,0:T(8,128)(2,1)S(1)} %fusion.42), kind=kOutput, calls=%fused_computation.8.clone.1 | convolution fusion | flops 1077936128 | bytes 2654208 | tf_op jit(solution)/shard_map/while/body/eval_jaxpr/dot_general | solution.py:21
  20.8 0.3 fusion.44
  21.1 0.6 broadcast.86
  21.7 0.7 reduce.3
  22.5 71.8 %all_gather.3 = bf16[64,24,128]{2,1,0:T(8,128)(2,1)S(1)} all-gather(bf16[2,24,128]{2,1,0:T(8,128)(2,1)S(1)} %copy-done.2), channel_id=1, replica_groups=mesh['pages'=8,'blocks'=4] {'pages','blocks'}, dimensions={0}, use_global_device_ids=true | all-gather | bytes 405504 | tf_op jit(solution)/shard_map/all_gather | solution.py:44
  94.3 38.7 %while.22 = (s32[]{:T(128)}, bf16[4,16,16,24]{3,2,1,0:T(8,128)(2,1)S(1)}, s32[4,16]{1,0:T(4,128)S(1)}, s32[4,16,16]{2,1,0:T(8,128)S(1)}, s32[1,32]{1,0:T(1,128)S...) while((s32[]{:T(128)}, ...), condition=%wide.region_5.6_spmd.clone, body=%wide.region_2.5_spmd.clone.sunk | while | flops 103591232 | bytes 12894645 | solution.py:63
  94.3 0.4 select_reduce_fusion.4
  95.0 3.0 %gather_fusion = bf16[256,64,128]{2,1,0:T(8,128)(2,1)} fusion(bf16[32,64,128]{2,1,0:T(8,128)(2,1)S(1)} %get-tuple-element.300, s32[1024]{0:T(1024)S(1)} %pad_clamp_fusion.2), kind=kCustom, calls=%fused_computation.clone.clone.1 | custom fusion | bytes 8389632 | tf_op jit(solution)/shard_map/while/body/eval_jaxpr/jit(_take)/gather | solution.py:50
  98.0 5.7 %select_reduce_fusion.5 = bf16[16,16,24]{2,1,0:T(8,128)(2,1)S(1)} fusion(pred[16,16,64]{2,1,0:T(8,128)(4,1)S(1)} %broadcast_compare_fusion.2, bf16[16,16,64,128]{3,2,1,0:T(8,128)(2,1)} %bitcast.62, pred[16,16]{1,0:T(8,128)(4,1)S(1)} %get-tuple-element.255, bf16[4,16,24,128]{3,2,1,0:T(8,128)(2,1)S(1)} %get-tuple-element.301, s32[]{:T(128)} %get-tuple-element.286), kind=kOutput, calls=%fused_computation.19.clone.1 | convolution fusion | flops 103540736 | bytes 4339716 | tf_op jit(solution)/shard_map/while/body/eval_jaxpr/gcpd,gtd->gcpt/dot_general | solution.py:51
  104.0 0.4 select_reduce_fusion.4
  104.7 3.0 %gather_fusion = bf16[256,64,128]{2,1,0:T(8,128)(2,1)} fusion(bf16[32,64,128]{2,1,0:T(8,128)(2,1)S(1)} %get-tuple-element.300, s32[1024]{0:T(1024)S(1)} %pad_clamp_fusion.2), kind=kCustom, calls=%fused_computation.clone.clone.1 | custom fusion | bytes 8389632 | tf_op jit(solution)/shard_map/while/body/eval_jaxpr/jit(_take)/gather | solution.py:50
  107.7 5.7 %select_reduce_fusion.5 = bf16[16,16,24]{2,1,0:T(8,128)(2,1)S(1)} fusion(pred[16,16,64]{2,1,0:T(8,128)(4,1)S(1)} %broadcast_compare_fusion.2, bf16[16,16,64,128]{3,2,1,0:T(8,128)(2,1)} %bitcast.62, pred[16,16]{1,0:T(8,128)(4,1)S(1)} %get-tuple-element.255, bf16[4,16,24,128]{3,2,1,0:T(8,128)(2,1)S(1)} %get-tuple-element.301, s32[]{:T(128)} %get-tuple-element.286), kind=kOutput, calls=%fused_computation.19.clone.1 | convolution fusion | flops 103540736 | bytes 4339716 | tf_op jit(solution)/shard_map/while/body/eval_jaxpr/gcpd,gtd->gcpt/dot_general | solution.py:51
  113.7 0.4 select_reduce_fusion.4
  114.3 3.0 %gather_fusion = bf16[256,64,128]{2,1,0:T(8,128)(2,1)} fusion(bf16[32,64,128]{2,1,0:T(8,128)(2,1)S(1)} %get-tuple-element.300, s32[1024]{0:T(1024)S(1)} %pad_clamp_fusion.2), kind=kCustom, calls=%fused_computation.clone.clone.1 | custom fusion | bytes 8389632 | tf_op jit(solution)/shard_map/while/body/eval_jaxpr/jit(_take)/gather | solution.py:50
  117.4 5.7 %select_reduce_fusion.5 = bf16[16,16,24]{2,1,0:T(8,128)(2,1)S(1)} fusion(pred[16,16,64]{2,1,0:T(8,128)(4,1)S(1)} %broadcast_compare_fusion.2, bf16[16,16,64,128]{3,2,1,0:T(8,128)(2,1)} %bitcast.62, pred[16,16]{1,0:T(8,128)(4,1)S(1)} %get-tuple-element.255, bf16[4,16,24,128]{3,2,1,0:T(8,128)(2,1)S(1)} %get-tuple-element.301, s32[]{:T(128)} %get-tuple-element.286), kind=kOutput, calls=%fused_computation.19.clone.1 | convolution fusion | flops 103540736 | bytes 4339716 | tf_op jit(solution)/shard_map/while/body/eval_jaxpr/gcpd,gtd->gcpt/dot_general | solution.py:51
  123.4 0.4 select_reduce_fusion.4
  124.0 3.0 %gather_fusion = bf16[256,64,128]{2,1,0:T(8,128)(2,1)} fusion(bf16[32,64,128]{2,1,0:T(8,128)(2,1)S(1)} %get-tuple-element.300, s32[1024]{0:T(1024)S(1)} %pad_clamp_fusion.2), kind=kCustom, calls=%fused_computation.clone.clone.1 | custom fusion | bytes 8389632 | tf_op jit(solution)/shard_map/while/body/eval_jaxpr/jit(_take)/gather | solution.py:50
  127.0 5.7 %select_reduce_fusion.5 = bf16[16,16,24]{2,1,0:T(8,128)(2,1)S(1)} fusion(pred[16,16,64]{2,1,0:T(8,128)(4,1)S(1)} %broadcast_compare_fusion.2, bf16[16,16,64,128]{3,2,1,0:T(8,128)(2,1)} %bitcast.62, pred[16,16]{1,0:T(8,128)(4,1)S(1)} %get-tuple-element.255, bf16[4,16,24,128]{3,2,1,0:T(8,128)(2,1)S(1)} %get-tuple-element.301, s32[]{:T(128)} %get-tuple-element.286), kind=kOutput, calls=%fused_computation.19.clone.1 | convolution fusion | flops 103540736 | bytes 4339716 | tf_op jit(solution)/shard_map/while/body/eval_jaxpr/gcpd,gtd->gcpt/dot_general | solution.py:51
  133.0 0.3 reshape.142
  133.4 8.2 %all_to_all.10 = bf16[8,2,1536]{2,1,0:T(2,128)(2,1)S(1)} all-to-all(bf16[8,2,1536]{2,1,0:T(2,128)(2,1)S(1)} %reshape.142), channel_id=1, replica_groups=mesh['pages'=8,'blocks'=4] {'pages'}, dimensions={0} | all-to-all | bytes 98304 | tf_op jit(solution)/shard_map/all_to_all | solution.py:77
  141.6 0.4 reshape.143
  142.0 0.3 reshape.144
  142.3 7.2 %all_to_all.11 = bf16[4,2,3072]{2,1,0:T(2,128)(2,1)S(1)} all-to-all(bf16[4,2,3072]{2,1,0:T(2,128)(2,1)S(1)} %reshape.144), channel_id=1, replica_groups=mesh['pages'=8,'blocks'=4] {'blocks'}, dimensions={0} | all-to-all | bytes 98304 | tf_op jit(solution)/shard_map/all_to_all | solution.py:76
  149.5 0.4 reshape.145
  150.0 0.6 copy.25
  (67 shorter events, 2.9 us)
Async XLA Ops:
  0.0 2.4 %copy-start = (bf16[256,128]{1,0:T(8,128)(2,1)S(1)}, bf16[256,128]{1,0:T(8,128)(2,1)}, u32[]{:S(2)}) copy-start(bf16[256,128]{1,0:T(8,128)(2,1)} %param.13) | copy-start | bytes 196612
  2.5 19.2 %copy-start.4 = (s32[1,64]{1,0:T(1,128)S(1)}, s32[1,64]{1,0:T(1,128)}, u32[]{:S(2)}) copy-start(s32[1,64]{1,0:T(1,128)} %param.19) | copy-start | bytes 772
  2.5 20.0 %copy-start.2 = (bf16[2,24,128]{2,1,0:T(8,128)(2,1)S(1)}, bf16[2,24,128]{2,1,0:T(8,128)(2,1)}, u32[]{:S(2)}) copy-start(bf16[2,24,128]{2,1,0:T(8,128)(2,1)} %param.12) | copy-start | bytes 36868
  2.5 91.7 %copy-start.3 = (s32[1,64,16]{1,2,0:T(8,128)S(1)}, s32[1,64,16]{1,2,0:T(8,128)}, u32[]{:S(2)}) copy-start(s32[1,64,16]{1,2,0:T(8,128)} %param.18) | copy-start | bytes 12292
  2.5 91.8 %copy-start.1 = (s32[1,32]{1,0:T(1,128)S(1)}, s32[1,32]{1,0:T(1,128)}, u32[]{:S(2)}) copy-start(s32[1,32]{1,0:T(1,128)} %param.17) | copy-start | bytes 388
where the time goes:
time: 151 us
  blocking collectives  87.1 us (58%)
  matrix products  33.6 us (22%)
  local copies, waits for them, and re-layouts  24.8 us (16%)
  other arithmetic  4.45 us (3%)
    all_gather x1, blocking collectives, on_device(): piece = lax.all_gather(queries, ('pages', 'blocks'), axis=0, tiled=True)  71.8 us
    dot_general x4, matrix products, one_block(): jnp.einsum('gcpd,gtd->gcpt', chosen, query_group, preferred_element_type=...  23 us
    gather x4, local copies, waits for them, and re-layouts, one_block(): chosen = jnp.take(embedded, cand_group, axis=0)  12.1 us
    dot_general x4, matrix products, decode_block(): jnp.dot(weighted, basis.reshape(cent_total * rank_width, width), preferre...  9.53 us
    all_to_all x1, blocking collectives, on_device(): lax.all_to_all(shaped, 'pages', split_axis=0, concat_axis=0, tiled=True)  8.2 us
    all_to_all x1, blocking collectives, on_device(): lax.all_to_all(lax.all_to_all(shaped, 'pages', split_axis=0, concat_axis=...  7.16 us
    dynamic_slice x8, local copies, waits for them, and re-layouts, on_device(): lax.map(lambda inputs: decode_block(inputs[0], inputs[1], centroids, basi...  5.83 us

commit v1 on v0

v1 whole, which is shorter than its diff:
```python
import functools

import jax
import jax.numpy as jnp
from jax import lax
from jax.experimental import pallas as pl
from jax.experimental.pallas import tpu as pltpu
from jax.sharding import PartitionSpec as P

MESH = pl.DeviceIdType.MESH
SPLIT = 2
STEP = 8
LOWEST = -3.0e38


def remote(src, dst, send, recv, where):
    return pltpu.make_async_remote_copy(
        src_ref=src, dst_ref=dst, send_sem=send, recv_sem=recv, device_id=where, device_id_type=MESH
    )


def kernel(
    n_pages, n_blocks, qtok,
    q_hbm, cent_hbm, basis_hbm, ids_hbm, coef_hbm, count_hbm, cand_hbm, live_hbm, out_ref,
    cent, basis, ids, coef, count, cand, live,
    qbuf, idb, dlow, emb, first, bound, outgo, income, scoreT, piece, landed,
    in_sem, z_send, z_recv, b_send, b_recv, c_send, c_recv, d_send, d_recv, e_send, e_recv,
):
    k = lax.axis_index("pages")
    r = lax.axis_index("blocks")
    core = lax.rem(k, 2)
    z = lax.div(k, 2)
    nz = n_pages // 2
    pages, patches = ids.shape
    cents, width = cent.shape
    rank = basis.shape[0] // cents
    rows_q = q_hbm.shape[0]
    cols = n_pages * rows_q

    barrier = pltpu.get_barrier_semaphore()
    for s in range(1, n_pages):
        pl.semaphore_signal(
            barrier, inc=1, device_id=(lax.rem(k + s, n_pages), r), device_id_type=MESH
        )
    for s in range(1, n_blocks):
        pl.semaphore_signal(
            barrier, inc=1, device_id=(k, lax.rem(r + s, n_blocks)), device_id_type=MESH
        )

    own = qbuf.at[r, core, pl.ds(pl.multiple_of(z * rows_q, rows_q), rows_q), :]
    loads = [
        pltpu.make_async_copy(src, dst, in_sem.at[i])
        for i, (src, dst) in enumerate(
            [
                (ids_hbm, ids), (count_hbm, count), (q_hbm, own), (coef_hbm, coef),
                (cent_hbm, cent), (basis_hbm, basis), (cand_hbm, cand), (live_hbm, live),
            ]
        )
    ]
    for copy in loads:
        copy.start()

    loads[0].wait()
    loads[1].wait()
    low_total = cents // SPLIT
    lane = lax.broadcasted_iota(jnp.int32, (pages, width), 1)
    lane_cent = lax.div(lane, rank)
    for p in range(patches):
        wide = jnp.broadcast_to(ids[:, p : p + 1], (pages, width))
        idb[p] = wide.astype(jnp.float32).astype(jnp.bfloat16)
        dlow[p] = (
            (lax.bitwise_and(wide, low_total - 1) - lane_cent).astype(jnp.float32).astype(jnp.bfloat16)
        )
    spread = jnp.broadcast_to(count[...].astype(jnp.float32), (pages, pages))
    diag = lax.broadcasted_iota(jnp.int32, (pages, pages), 0) == lax.broadcasted_iota(
        jnp.int32, (pages, pages), 1
    )
    column = jnp.sum(jnp.where(diag, spread, 0.0), axis=1, keepdims=True)
    bound[...] = jnp.broadcast_to(column, (pages, width)) - (r * patches).astype(jnp.float32)

    loads[2].wait()
    pl.semaphore_wait(barrier, n_pages - 1 + n_blocks - 1)
    z_copies = []
    for s in range(1, nz):
        to = lax.rem(z + s, nz)
        z_copies.append(
            remote(own, own, z_send.at[s], z_recv.at[s], (to * 2 + core, r))
        )
    for copy in z_copies:
        copy.start()

    for copy in loads[3:]:
        copy.wait()

    per = width // rank
    tile_row = lax.broadcasted_iota(jnp.int32, (width, per * width), 0)
    tile_col = lax.broadcasted_iota(jnp.int32, (width, per * width), 1)
    tile = (
        (tile_row == lax.div(tile_col, width) * rank + lax.rem(tile_col, rank))
        .astype(jnp.float32)
        .astype(jnp.bfloat16)
    )
    depth = low_total * rank
    rows = STEP * pages

    def decode(m):
        base = m * STEP
        parts = []
        for h in range(STEP // per):
            chunk = coef[:, pl.ds(pl.multiple_of((m * (STEP // per) + h) * width, width), width)]
            spreadc = jnp.dot(chunk, tile, preferred_element_type=jnp.float32)
            for s in range(per):
                parts.append(spreadc[:, s * width : (s + 1) * width].astype(jnp.bfloat16))
        weights = jnp.concatenate(parts, axis=0)
        low = dlow[pl.ds(base, STEP)].reshape(rows, width)
        mine = idb[pl.ds(base, STEP)].reshape(rows, width)
        zero = jnp.zeros((rows, width), jnp.bfloat16)
        lhs = jnp.concatenate(
            [
                jnp.where(low == jnp.bfloat16(per * t), weights, zero)
                for t in range(depth // width)
            ],
            axis=1,
        )
        rhs = jnp.concatenate(
            [basis[h * depth : (h + 1) * depth, :] for h in range(SPLIT)], axis=1
        )
        res = jnp.dot(lhs, rhs, preferred_element_type=jnp.float32)
        lane_id = lax.broadcasted_iota(jnp.int32, (rows, width), 1).astype(jnp.float32).astype(jnp.bfloat16)
        one = jnp.ones((rows, width), jnp.bfloat16)
        hot = jnp.concatenate(
            [
                jnp.where(mine == lane_id + jnp.bfloat16(t * width), one, zero)
                for t in range(cents // width)
            ],
            axis=1,
        )
        center = jnp.dot(hot, cent[...], preferred_element_type=jnp.float32)
        mine_f = mine.astype(jnp.float32)
        total = res[:, :width]
        for h in range(1, SPLIT):
            total = jnp.where(
                mine_f >= float(h * low_total), res[:, h * width : (h + 1) * width], total
            )
        total = (total + center).reshape(STEP, pages, width)

        @pl.when(m == 0)
        def _():
            first[...] = total[0]

        position = base + lax.broadcasted_iota(jnp.int32, (STEP, pages, width), 0)
        valid = position.astype(jnp.float32) < bound[...][None]
        total = jnp.where(valid, total, first[...][None])
        emb[pl.ds(pl.multiple_of(m * rows, rows), rows), :] = total.astype(jnp.bfloat16).reshape(rows, width)

    turns = patches // STEP
    half = turns // 2

    def decode_step(m, carry):
        decode(m)
        return carry

    lax.fori_loop(0, half, decode_step, 0)

    partner = (k + 1 - 2 * core, r)
    for copy in z_copies:
        copy.wait_recv()
    b_copies = []
    for s in range(1, n_blocks):
        to = lax.rem(r + s, n_blocks)
        b_copies.append(
            remote(qbuf.at[r, core], qbuf.at[r, core], b_send.at[s], b_recv.at[s], (k, to))
        )
    for copy in b_copies:
        copy.start()
    c_copies = [
        remote(qbuf.at[r, core], qbuf.at[r, core], c_send.at[0], c_recv.at[0], partner)
    ]
    c_copies[0].start()

    lax.fori_loop(half, turns, decode_step, 0)

    for s in range(1, n_blocks):
        b_copies[s - 1].wait_recv()
        source = lax.rem(r + n_blocks - s, n_blocks)
        copy = remote(
            qbuf.at[source, core], qbuf.at[source, core], c_send.at[s], c_recv.at[s], partner
        )
        copy.start()
        c_copies.append(copy)

    def best_of(source):
        query = qbuf[source].reshape(cols, width)

        def more(m, best):
            block = emb[pl.ds(pl.multiple_of(m * rows, rows), rows), :]
            sim = lax.dot_general(
                block, query, (((1,), (1,)), ((), ())), preferred_element_type=jnp.float32
            )
            return jnp.maximum(best, jnp.max(sim.reshape(STEP, pages, cols), axis=0))

        best = lax.fori_loop(0, turns, more, jnp.full((pages, cols), LOWEST, jnp.float32))
        return jnp.where(bound[:, :1] > 0.0, best, LOWEST).astype(jnp.bfloat16)

    d_copies = []
    for s in range(n_blocks):
        c_copies[s].wait_recv()
        source = lax.rem(r + n_blocks - s, n_blocks)
        if s == 0:
            income[0] = best_of(source)
        else:
            outgo[s] = best_of(source)
            copy = remote(outgo.at[s], income.at[s], d_send.at[s], d_recv.at[s], (k, source))
            copy.start()
            d_copies.append(copy)

    n_query = cand.shape[1]
    per_dev = rows_q // qtok
    spot = lax.broadcasted_iota(jnp.int32, (cols, n_query), 0)
    seen = lax.broadcasted_iota(jnp.int32, (cols, n_query), 1)
    shard = lax.div(spot, rows_q)
    owner = lax.rem(shard, nz) * 2 + lax.div(shard, nz)
    index = (owner * n_blocks + r) * per_dev + lax.div(lax.rem(spot, rows_q), qtok)
    gather = (index == seen).astype(jnp.float32).astype(jnp.bfloat16)
    slots = cand.shape[0]
    used = lax.broadcasted_iota(jnp.int32, (slots, n_query), 0) < live[...]
    chosen = cand[...]

    highest = income[0].astype(jnp.float32)
    for copy in d_copies:
        copy.wait_recv()
    for s in range(1, n_blocks):
        highest = jnp.maximum(highest, income[s].astype(jnp.float32))
    sums = jnp.dot(highest.astype(jnp.bfloat16), gather, preferred_element_type=jnp.float32)
    picked = jnp.zeros((slots, n_query), jnp.float32)
    for n in range(pages):
        picked = jnp.where(chosen == n, sums[n : n + 1, :], picked)
    picked = jnp.where(used, picked / qtok, 0.0)
    wide_q = scoreT.shape[0]
    padded = picked
    if wide_q > n_query:
        padded = jnp.concatenate([padded, jnp.zeros((slots, wide_q - n_query), jnp.float32)], axis=1)
    full = jnp.concatenate([padded, jnp.zeros((width - slots, wide_q), jnp.float32)], axis=0)
    scoreT[...] = full.T

    e_copies = []
    for s in range(n_pages):
        to = lax.rem(k + s, n_pages)
        values = scoreT[pl.ds((to * n_blocks + r) * per_dev, per_dev), :]
        if s == 0:
            landed[k] = values
        else:
            piece[s] = values
            copy = remote(piece.at[s], landed.at[k], e_send.at[s], e_recv.at[s], (to, r))
            copy.start()
            e_copies.append(copy)
    for copy in e_copies:
        copy.wait_recv()
    for g in range(n_pages):
        arrived = landed[g]
        for i in range(per_dev):
            out_ref[i, g : g + 1, :] = arrived[i : i + 1, :slots]
    for copy in z_copies + b_copies + c_copies + d_copies + e_copies:
        copy.wait_send()


def on_device(queries, centroids, basis, patch_ids, coeffs, page_counts, cand_ids, cand_counts):
    n_pages = lax.axis_size("pages")
    n_blocks = lax.axis_size("blocks")
    owned, qtok, width = queries.shape
    cents, rank, _ = basis.shape
    _, pages, patches = patch_ids.shape
    _, n_query, slots = cand_ids.shape
    rows_q = owned * qtok
    cols = n_pages * rows_q
    args = (
        queries.reshape(rows_q, width),
        centroids,
        basis.reshape(cents * rank, width),
        patch_ids[0],
        coeffs[0],
        page_counts,
        jnp.swapaxes(cand_ids[0], 0, 1),
        cand_counts,
    )
    dma = pltpu.SemaphoreType.DMA
    bf16, f32 = jnp.bfloat16, jnp.float32
    vmem = pltpu.VMEM
    return pl.pallas_call(
        functools.partial(kernel, n_pages, n_blocks, qtok),
        out_shape=jax.ShapeDtypeStruct((owned, n_pages, slots), f32),
        in_specs=[pl.BlockSpec(memory_space=pl.ANY)] * len(args),
        out_specs=pl.BlockSpec(memory_space=pltpu.VMEM),
        scratch_shapes=[vmem(a.shape, a.dtype) for a in args[1:]]
        + [
            vmem((n_blocks, 2, cols // 2, width), bf16),
            vmem((patches, pages, width), bf16),
            vmem((patches, pages, width), bf16),
            vmem((patches * pages, width), bf16),
            vmem((pages, width), f32),
            vmem((pages, width), f32),
            vmem((n_blocks, pages, cols), bf16),
            vmem((n_blocks, pages, cols), bf16),
            vmem((-(-n_query // 128) * 128, width), f32),
            vmem((n_pages, owned, width), f32),
            vmem((n_pages, owned, width), f32),
            dma((len(args),)),
            dma((n_pages,)), dma((n_pages,)),
            dma((n_blocks,)), dma((n_blocks,)),
            dma((n_blocks,)), dma((n_blocks,)),
            dma((n_blocks,)), dma((n_blocks,)),
            dma((n_pages,)), dma((n_pages,)),
        ],
        compiler_params=pltpu.CompilerParams(collective_id=0, has_side_effects=True),
    )(*args)


def solution(mesh):
    placed = (
        P(("pages", "blocks"), None, None),
        P(),
        P(),
        P("pages", None, "blocks"),
        P("pages", None, "blocks"),
        P("pages", None),
        P("pages", None, None),
        P("pages", None),
    )
    return jax.shard_map(
        on_device,
        mesh=mesh,
        in_specs=placed,
        out_specs=P(("pages", "blocks"), None, None),
        check_vma=False,
    )
```

time: 151 us -> 30.9 us (0.20)
  blocking collectives: 87.1 us -> 0 us
  matrix products: 33.6 us -> 0 us
  Pallas kernels: 0 us -> 29.3 us
  local copies, waits for them, and re-layouts: 24.8 us -> 1.3 us
  other arithmetic: 4.45 us -> 0 us
    all_gather x1 -> x0, blocking collectives: 71.8 us -> none  [on_device(): piece = lax.all_gather(queries, ('pages', 'blocks'), axis=0, tiled=True)]
    dot_general x12 -> x0, matrix products: 33.6 us -> none  [the longest x4 23 us: one_block(): jnp.einsum('gcpd,gtd->gcpt', chosen, query_group, preferred_element_type=...]
    pallas_call x0 -> x1, Pallas kernels: none -> 29.3 us  [on_device(): pl.pallas_call(functools.partial(kernel, n_pages, n_blocks, qtok), out_sh...]
    all_to_all x2 -> x0, blocking collectives: 15.4 us -> none  [the longest x1 8.2 us: on_device(): lax.all_to_all(shaped, 'pages', split_axis=0, concat_axis=0, tiled=True)]
    gather x4 -> x0, local copies, waits for them, and re-layouts: 12.1 us -> none  [one_block(): chosen = jnp.take(embedded, cand_group, axis=0)]
    dynamic_slice x8 -> x0, local copies, waits for them, and re-layouts: 5.83 us -> none  [on_device(): lax.map(lambda inputs: decode_block(inputs[0], inputs[1], centroids, basi...]
    while x1 -> x0, local copies, waits for them, and re-layouts: 2.43 us -> none  [on_device(): lax.map(lambda inputs: decode_block(inputs[0], inputs[1], centroids, basi...]
    reduce_sum x5 -> x0, other arithmetic: 1.82 us -> none  [the longest x4 1.7 us: one_block(): jnp.sum(jnp.where(match_page, live_counts[None, None, :], 0), axis=2)]
where the time goes in v1:
time: 30.9 us; the launch traced here: 30.7 us
  Pallas kernels  29.3 us (95%)
  local copies, waits for them, and re-layouts  1.3 us (4%)
    pallas_call x1, Pallas kernels, on_device(): pl.pallas_call(functools.partial(kernel, n_pages, n_blocks, qtok), out_sh...  29.3 us
    unnamed x1, local copies, waits for them, and re-layouts  1.3 us

profile of v1, /device:TPU:0, one launch (start us, length us, event | category | flops | bytes accessed | tf_op | source)
XLA Modules:
  0.0 30.7 jit_solution(6635705917207720868)
XLA Ops:
  0.0 29.3 %shard_map.82 = f32[2,8,16]{2,1,0:T(8,128)} custom-call(bf16[48,128]{1,0:T(8,128)(2,1)} %bitcast.10, bf16[256,128]{1,0:T(8,128)(2,1)} %cent_hbm.1, bf16[8192,128]{1,0:T(8,128)(2,1)} %bitcast.7, s32[32,64]{1,0:T(8,128)} %bitcast.9, bf16[32,2048]{1,0:T(8,128)(2,1)} %bitcast.8, s32[1,32]{1,0:T(1,128)} %count_hbm.1, s32[16,64]{1,0:T(8,128)} %bitcast.11, ...), custom_call_target="tpu_custom_call" | custom-call | tf_op jit(solution)/shard_map/pallas_call | solution.py:289
  29.4 1.3 %copy.10 = f32[2,8,16]{2,1,0:T(8,128)} copy(f32[2,8,16]{2,1,0:T(8,128)} %shard_map.82) | data formatting | bytes 2048

commit v2 on v1

--- a/solution.py
+++ b/solution.py
@@ -8,8 +8,9 @@
 from jax.sharding import PartitionSpec as P
 
 MESH = pl.DeviceIdType.MESH
-SPLIT = 2
+SPLIT = 4
 STEP = 8
+AHEAD, NEAR, FAR = 1, 3, 4
 LOWEST = -3.0e38
 
 
@@ -17,13 +18,24 @@
     return pltpu.make_async_remote_copy(
         src_ref=src, dst_ref=dst, send_sem=send, recv_sem=recv, device_id=where, device_id_type=MESH
     )
+
+
+def flip(index, bits):
+    for bit in range(bits.bit_length()):
+        if bits >> bit & 1:
+            index = index + 2**bit - 2 ** (bit + 1) * lax.rem(lax.div(index, 2**bit), 2)
+    return index
+
+
+def far_first(count):
+    return sorted(range(1, count), key=lambda s: -s.bit_count())
 
 
 def kernel(
     n_pages, n_blocks, qtok,
     q_hbm, cent_hbm, basis_hbm, ids_hbm, coef_hbm, count_hbm, cand_hbm, live_hbm, out_ref,
     cent, basis, ids, coef, count, cand, live,
-    qbuf, idb, dlow, emb, first, bound, outgo, income, scoreT, piece, landed,
+    qbuf, idb, dlow, emb, first, bound, outgo, income, gather, scoreT, piece, landed,
     in_sem, z_send, z_recv, b_send, b_recv, c_send, c_recv, d_send, d_recv, e_send, e_recv,
 ):
     k = lax.axis_index("pages")
@@ -63,14 +75,21 @@
     loads[0].wait()
     loads[1].wait()
     low_total = cents // SPLIT
-    lane = lax.broadcasted_iota(jnp.int32, (pages, width), 1)
-    lane_cent = lax.div(lane, rank)
-    for p in range(patches):
-        wide = jnp.broadcast_to(ids[:, p : p + 1], (pages, width))
-        idb[p] = wide.astype(jnp.float32).astype(jnp.bfloat16)
-        dlow[p] = (
-            (lax.bitwise_and(wide, low_total - 1) - lane_cent).astype(jnp.float32).astype(jnp.bfloat16)
-        )
+    lane_cent = lax.div(lax.broadcasted_iota(jnp.int32, (pages, STEP * width), 1), rank)
+    lane_cent = lax.rem(lane_cent, width // rank).astype(jnp.float32)
+    id_f = ids[...].astype(jnp.float32)
+    id_low = lax.bitwise_and(ids[...], low_total - 1).astype(jnp.float32)
+    id_both = jnp.concatenate([id_f, id_low], axis=0).astype(jnp.bfloat16)
+    from_row = lax.broadcasted_iota(jnp.int32, (patches, STEP * width), 0)
+    to_col = lax.div(lax.broadcasted_iota(jnp.int32, (patches, STEP * width), 1), width)
+    for m in range(patches // STEP):
+        pick = (from_row == to_col + m * STEP).astype(jnp.float32).astype(jnp.bfloat16)
+        wide = jnp.dot(id_both, pick, preferred_element_type=jnp.float32)
+        wide_id = wide[:pages].astype(jnp.bfloat16)
+        wide_low = (wide[pages:] - lane_cent).astype(jnp.bfloat16)
+        for p in range(STEP):
+            idb[m * STEP + p] = wide_id[:, p * width : (p + 1) * width]
+            dlow[m * STEP + p] = wide_low[:, p * width : (p + 1) * width]
     spread = jnp.broadcast_to(count[...].astype(jnp.float32), (pages, pages))
     diag = lax.broadcasted_iota(jnp.int32, (pages, pages), 0) == lax.broadcasted_iota(
         jnp.int32, (pages, pages), 1
@@ -78,19 +97,17 @@
     column = jnp.sum(jnp.where(diag, spread, 0.0), axis=1, keepdims=True)
     bound[...] = jnp.broadcast_to(column, (pages, width)) - (r * patches).astype(jnp.float32)
 
-    loads[2].wait()
-    pl.semaphore_wait(barrier, n_pages - 1 + n_blocks - 1)
-    z_copies = []
-    for s in range(1, nz):
-        to = lax.rem(z + s, nz)
-        z_copies.append(
-            remote(own, own, z_send.at[s], z_recv.at[s], (to * 2 + core, r))
-        )
-    for copy in z_copies:
-        copy.start()
-
     for copy in loads[3:]:
         copy.wait()
+
+    n_query = cand.shape[1]
+    per_dev = rows_q // qtok
+    spot = lax.broadcasted_iota(jnp.int32, (cols, n_query), 0)
+    seen = lax.broadcasted_iota(jnp.int32, (cols, n_query), 1)
+    shard = lax.div(spot, rows_q)
+    owner = lax.rem(shard, nz) * 2 + lax.div(shard, nz)
+    index = (owner * n_blocks + r) * per_dev + lax.div(lax.rem(spot, rows_q), qtok)
+    gather[...] = (index == seen).astype(jnp.float32).astype(jnp.bfloat16)
 
     per = width // rank
     tile_row = lax.broadcasted_iota(jnp.int32, (width, per * width), 0)
@@ -154,74 +171,82 @@
         emb[pl.ds(pl.multiple_of(m * rows, rows), rows), :] = total.astype(jnp.bfloat16).reshape(rows, width)
 
     turns = patches // STEP
-    half = turns // 2
-
-    def decode_step(m, carry):
-        decode(m)
-        return carry
-
-    lax.fori_loop(0, half, decode_step, 0)
-
+
+    def decode_steps(start, stop):
+        start, stop = min(start, turns), min(stop, turns)
+        if stop > start:
+            lax.fori_loop(start, stop, lambda m, carry: (decode(m), carry)[1], 0)
+
+    def shard_at(block, where):
+        return qbuf.at[block, core, pl.ds(pl.multiple_of(where * rows_q, rows_q), rows_q), :]
+
+    decode_steps(0, AHEAD)
+    loads[2].wait()
+    pl.semaphore_wait(barrier, n_pages - 1 + n_blocks - 1)
+    z_copies = {
+        s: remote(own, own, z_send.at[s], z_recv.at[s], (flip(z, s) * 2 + core, r))
+        for s in far_first(nz)
+    }
+    for copy in z_copies.values():
+        copy.start()
+    b_copies = {}
+
+    def forward(t):
+        if t:
+            z_copies[t].wait_recv()
+        part = shard_at(r, flip(z, t))
+        for s in far_first(n_blocks):
+            b_copies[s, t] = remote(
+                part, part, b_send.at[s, t], b_recv.at[s, t], (k, flip(r, s))
+            )
+            b_copies[s, t].start()
+
+    forward(0)
+    decode_steps(AHEAD, NEAR)
+    for t in range(1, nz // 2 + 1):
+        forward(t)
+    decode_steps(NEAR, FAR)
+    for t in range(nz // 2 + 1, nz):
+        forward(t)
     partner = (k + 1 - 2 * core, r)
-    for copy in z_copies:
-        copy.wait_recv()
-    b_copies = []
-    for s in range(1, n_blocks):
-        to = lax.rem(r + s, n_blocks)
-        b_copies.append(
-            remote(qbuf.at[r, core], qbuf.at[r, core], b_send.at[s], b_recv.at[s], (k, to))
-        )
-    for copy in b_copies:
+
+    def share(s):
+        for t in range(nz):
+            if s:
+                b_copies[s, t].wait_recv()
+        half = qbuf.at[flip(r, s), core]
+        copy = remote(half, half, c_send.at[s], c_recv.at[s], partner)
         copy.start()
-    c_copies = [
-        remote(qbuf.at[r, core], qbuf.at[r, core], c_send.at[0], c_recv.at[0], partner)
-    ]
-    c_copies[0].start()
-
-    lax.fori_loop(half, turns, decode_step, 0)
-
-    for s in range(1, n_blocks):
-        b_copies[s - 1].wait_recv()
-        source = lax.rem(r + n_blocks - s, n_blocks)
-        copy = remote(
-            qbuf.at[source, core], qbuf.at[source, core], c_send.at[s], c_recv.at[s], partner
-        )
-        copy.start()
-        c_copies.append(copy)
+        return copy
+
+    c_copies = {0: share(0)}
+    decode_steps(FAR, turns)
 
     def best_of(source):
         query = qbuf[source].reshape(cols, width)
 
-        def more(m, best):
-            block = emb[pl.ds(pl.multiple_of(m * rows, rows), rows), :]
+        best = jnp.full((pages, cols), LOWEST, jnp.float32)
+        for m in range(turns):
             sim = lax.dot_general(
-                block, query, (((1,), (1,)), ((), ())), preferred_element_type=jnp.float32
+                emb[m * rows : (m + 1) * rows, :], query, (((1,), (1,)), ((), ())),
+                preferred_element_type=jnp.float32,
             )
-            return jnp.maximum(best, jnp.max(sim.reshape(STEP, pages, cols), axis=0))
-
-        best = lax.fori_loop(0, turns, more, jnp.full((pages, cols), LOWEST, jnp.float32))
+            best = jnp.maximum(best, jnp.max(sim.reshape(STEP, pages, cols), axis=0))
         return jnp.where(bound[:, :1] > 0.0, best, LOWEST).astype(jnp.bfloat16)
 
+    c_copies[0].wait_recv()
+    income[0] = best_of(r)
+    for s in far_first(n_blocks):
+        c_copies[s] = share(s)
     d_copies = []
-    for s in range(n_blocks):
+    for s in far_first(n_blocks):
         c_copies[s].wait_recv()
-        source = lax.rem(r + n_blocks - s, n_blocks)
-        if s == 0:
-            income[0] = best_of(source)
-        else:
-            outgo[s] = best_of(source)
-            copy = remote(outgo.at[s], income.at[s], d_send.at[s], d_recv.at[s], (k, source))
-            copy.start()
-            d_copies.append(copy)
-
-    n_query = cand.shape[1]
-    per_dev = rows_q // qtok
-    spot = lax.broadcasted_iota(jnp.int32, (cols, n_query), 0)
-    seen = lax.broadcasted_iota(jnp.int32, (cols, n_query), 1)
-    shard = lax.div(spot, rows_q)
-    owner = lax.rem(shard, nz) * 2 + lax.div(shard, nz)
-    index = (owner * n_blocks + r) * per_dev + lax.div(lax.rem(spot, rows_q), qtok)
-    gather = (index == seen).astype(jnp.float32).astype(jnp.bfloat16)
+        source = flip(r, s)
+        outgo[s] = best_of(source)
+        copy = remote(outgo.at[s], income.at[s], d_send.at[s], d_recv.at[s], (k, source))
+        copy.start()
+        d_copies.append(copy)
+
     slots = cand.shape[0]
     used = lax.broadcasted_iota(jnp.int32, (slots, n_query), 0) < live[...]
     chosen = cand[...]
@@ -231,11 +256,11 @@
         copy.wait_recv()
     for s in range(1, n_blocks):
         highest = jnp.maximum(highest, income[s].astype(jnp.float32))
-    sums = jnp.dot(highest.astype(jnp.bfloat16), gather, preferred_element_type=jnp.float32)
+    sums = jnp.dot(highest.astype(jnp.bfloat16), gather[...], preferred_element_type=jnp.float32)
     picked = jnp.zeros((slots, n_query), jnp.float32)
     for n in range(pages):
         picked = jnp.where(chosen == n, sums[n : n + 1, :], picked)
-    picked = jnp.where(used, picked / qtok, 0.0)
+    picked = jnp.where(used, picked, 0.0)
     wide_q = scoreT.shape[0]
     padded = picked
     if wide_q > n_query:
@@ -244,8 +269,8 @@
     scoreT[...] = full.T
 
     e_copies = []
-    for s in range(n_pages):
-        to = lax.rem(k + s, n_pages)
+    for s in range(n_pages - 1, -1, -1):
+        to = flip(k, s)
         values = scoreT[pl.ds((to * n_blocks + r) * per_dev, per_dev), :]
         if s == 0:
             landed[k] = values
@@ -260,7 +285,8 @@
         arrived = landed[g]
         for i in range(per_dev):
             out_ref[i, g : g + 1, :] = arrived[i : i + 1, :slots]
-    for copy in z_copies + b_copies + c_copies + d_copies + e_copies:
+    started = [*z_copies.values(), *b_copies.values(), *c_copies.values(), *d_copies, *e_copies]
+    for copy in started:
         copy.wait_send()
 
 
@@ -286,7 +312,7 @@
     dma = pltpu.SemaphoreType.DMA
     bf16, f32 = jnp.bfloat16, jnp.float32
     vmem = pltpu.VMEM
-    return pl.pallas_call(
+    totals = pl.pallas_call(
         functools.partial(kernel, n_pages, n_blocks, qtok),
         out_shape=jax.ShapeDtypeStruct((owned, n_pages, slots), f32),
         in_specs=[pl.BlockSpec(memory_space=pl.ANY)] * len(args),
@@ -301,18 +327,20 @@
             vmem((pages, width), f32),
             vmem((n_blocks, pages, cols), bf16),
             vmem((n_blocks, pages, cols), bf16),
+            vmem((cols, n_query), bf16),
             vmem((-(-n_query // 128) * 128, width), f32),
             vmem((n_pages, owned, width), f32),
             vmem((n_pages, owned, width), f32),
             dma((len(args),)),
             dma((n_pages,)), dma((n_pages,)),
-            dma((n_blocks,)), dma((n_blocks,)),
+            dma((n_blocks, n_pages // 2)), dma((n_blocks, n_pages // 2)),
             dma((n_blocks,)), dma((n_blocks,)),
             dma((n_blocks,)), dma((n_blocks,)),
             dma((n_pages,)), dma((n_pages,)),
         ],
         compiler_params=pltpu.CompilerParams(collective_id=0, has_side_effects=True),
     )(*args)
+    return totals / qtok
 
 
 def solution(mesh):

time: 30.9 us -> 25.6 us (0.83)
  Pallas kernels: 29.3 us -> 24 us
  other arithmetic: 0 us -> 1.3 us
  local copies, waits for them, and re-layouts: 1.3 us -> 0 us
    pallas_call x1, Pallas kernels: 29.3 us -> 24 us  [on_device(): pl.pallas_call(functools.partial(kernel, n_pages, n_blocks, qtok), out_sh...]
    div x0 -> x1, other arithmetic: none -> 1.3 us  [on_device(): return totals / qtok]
    unnamed x1 -> x0, local copies, waits for them, and re-layouts: 1.3 us -> none
where the time goes in v2:
time: 25.6 us; the launch traced here: 25.3 us
  Pallas kernels  24 us (94%)
  other arithmetic  1.3 us (5%)
    pallas_call x1, Pallas kernels, on_device(): pl.pallas_call(functools.partial(kernel, n_pages, n_blocks, qtok), out_sh...  24 us
    div x1, other arithmetic, on_device(): return totals / qtok  1.3 us

profile of v2, /device:TPU:0, one launch (start us, length us, event | category | flops | bytes accessed | tf_op | source)
XLA Modules:
  0.0 25.3 jit_solution(14042008799544030268)
XLA Ops:
  0.0 24.0 %shard_map.82 = f32[2,8,16]{2,1,0:T(8,128)} custom-call(bf16[48,128]{1,0:T(8,128)(2,1)} %bitcast.10, bf16[256,128]{1,0:T(8,128)(2,1)} %cent_hbm.1, bf16[8192,128]{1,0:T(8,128)(2,1)} %bitcast.7, s32[32,64]{1,0:T(8,128)} %bitcast.9, bf16[32,2048]{1,0:T(8,128)(2,1)} %bitcast.8, s32[1,32]{1,0:T(1,128)} %count_hbm.1, s32[16,64]{1,0:T(8,128)} %bitcast.11, ...), custom_call_target="tpu_custom_call" | custom-call | tf_op jit(solution)/shard_map/pallas_call | solution.py:315
  24.0 1.3 %broadcast_multiply_fusion = f32[2,8,16]{2,1,0:T(8,128)} fusion(f32[2,8,16]{2,1,0:T(8,128)} %shard_map.82), kind=kLoop, calls=%fused_computation | loop fusion | flops 256 | bytes 2048 | tf_op jit(solution)/shard_map/div | solution.py:343

commit v3 on v2

--- a/solution.py
+++ b/solution.py
@@ -75,16 +75,18 @@
     loads[0].wait()
     loads[1].wait()
     low_total = cents // SPLIT
-    lane_cent = lax.div(lax.broadcasted_iota(jnp.int32, (pages, STEP * width), 1), rank)
+    lane_cent = lax.div(lax.broadcasted_iota(jnp.int32, (1, STEP * width), 1), rank)
     lane_cent = lax.rem(lane_cent, width // rank).astype(jnp.float32)
     id_f = ids[...].astype(jnp.float32)
     id_low = lax.bitwise_and(ids[...], low_total - 1).astype(jnp.float32)
     id_both = jnp.concatenate([id_f, id_low], axis=0).astype(jnp.bfloat16)
-    from_row = lax.broadcasted_iota(jnp.int32, (patches, STEP * width), 0)
-    to_col = lax.div(lax.broadcasted_iota(jnp.int32, (patches, STEP * width), 1), width)
+    to_col = lax.div(lax.broadcasted_iota(jnp.int32, (1, STEP * width), 1), width)
+    from_row = lax.broadcasted_iota(jnp.int32, (STEP, STEP * width), 0)
+    pick = (from_row == to_col).astype(jnp.float32).astype(jnp.bfloat16)
     for m in range(patches // STEP):
-        pick = (from_row == to_col + m * STEP).astype(jnp.float32).astype(jnp.bfloat16)
-        wide = jnp.dot(id_both, pick, preferred_element_type=jnp.float32)
+        wide = jnp.dot(
+            id_both[:, m * STEP : (m + 1) * STEP], pick, preferred_element_type=jnp.float32
+        )
         wide_id = wide[:pages].astype(jnp.bfloat16)
         wide_low = (wide[pages:] - lane_cent).astype(jnp.bfloat16)
         for p in range(STEP):
@@ -102,8 +104,8 @@
 
     n_query = cand.shape[1]
     per_dev = rows_q // qtok
-    spot = lax.broadcasted_iota(jnp.int32, (cols, n_query), 0)
-    seen = lax.broadcasted_iota(jnp.int32, (cols, n_query), 1)
+    spot = lax.broadcasted_iota(jnp.int32, (1, cols), 1)
+    seen = lax.broadcasted_iota(jnp.int32, (n_query, cols), 0)
     shard = lax.div(spot, rows_q)
     owner = lax.rem(shard, nz) * 2 + lax.div(shard, nz)
     index = (owner * n_blocks + r) * per_dev + lax.div(lax.rem(spot, rows_q), qtok)
@@ -111,7 +113,7 @@
 
     per = width // rank
     tile_row = lax.broadcasted_iota(jnp.int32, (width, per * width), 0)
-    tile_col = lax.broadcasted_iota(jnp.int32, (width, per * width), 1)
+    tile_col = lax.broadcasted_iota(jnp.int32, (1, per * width), 1)
     tile = (
         (tile_row == lax.div(tile_col, width) * rank + lax.rem(tile_col, rank))
         .astype(jnp.float32)
@@ -256,7 +258,10 @@
         copy.wait_recv()
     for s in range(1, n_blocks):
         highest = jnp.maximum(highest, income[s].astype(jnp.float32))
-    sums = jnp.dot(highest.astype(jnp.bfloat16), gather[...], preferred_element_type=jnp.float32)
+    sums = lax.dot_general(
+        highest.astype(jnp.bfloat16), gather[...], (((1,), (1,)), ((), ())),
+        preferred_element_type=jnp.float32,
+    )
     picked = jnp.zeros((slots, n_query), jnp.float32)
     for n in range(pages):
         picked = jnp.where(chosen == n, sums[n : n + 1, :], picked)
@@ -327,7 +332,7 @@
             vmem((pages, width), f32),
             vmem((n_blocks, pages, cols), bf16),
             vmem((n_blocks, pages, cols), bf16),
-            vmem((cols, n_query), bf16),
+            vmem((n_query, cols), bf16),
             vmem((-(-n_query // 128) * 128, width), f32),
             vmem((n_pages, owned, width), f32),
             vmem((n_pages, owned, width), f32),

time: 25.6 us -> 25.3 us (0.988)
  no operation moved by 1% of the time
where the time goes in v3:
time: 25.3 us; the launch traced here: 25.1 us
  Pallas kernels  23.8 us (94%)
  other arithmetic  1.3 us (5%)
    pallas_call x1, Pallas kernels, on_device(): pl.pallas_call(functools.partial(kernel, n_pages, n_blocks, qtok), out_sh...  23.8 us
    div x1, other arithmetic, on_device(): return totals / qtok  1.3 us

profile of v3, /device:TPU:0, one launch (start us, length us, event | category | flops | bytes accessed | tf_op | source)
XLA Modules:
  0.0 25.1 jit_solution(15816497644584306678)
XLA Ops:
  0.0 23.8 %shard_map.82 = f32[2,8,16]{2,1,0:T(8,128)} custom-call(bf16[48,128]{1,0:T(8,128)(2,1)} %bitcast.10, bf16[256,128]{1,0:T(8,128)(2,1)} %cent_hbm.1, bf16[8192,128]{1,0:T(8,128)(2,1)} %bitcast.7, s32[32,64]{1,0:T(8,128)} %bitcast.9, bf16[32,2048]{1,0:T(8,128)(2,1)} %bitcast.8, s32[1,32]{1,0:T(1,128)} %count_hbm.1, s32[16,64]{1,0:T(8,128)} %bitcast.11, ...), custom_call_target="tpu_custom_call" | custom-call | tf_op jit(solution)/shard_map/pallas_call | solution.py:320
  23.8 1.3 %broadcast_multiply_fusion = f32[2,8,16]{2,1,0:T(8,128)} fusion(f32[2,8,16]{2,1,0:T(8,128)} %shard_map.82), kind=kLoop, calls=%fused_computation | loop fusion | flops 256 | bytes 2048 | tf_op jit(solution)/shard_map/div | solution.py:348
